TPU v7x, 32 devices: a whole 2x2x4 slice. The times are simulated.
32 devices in a mesh: outer: 8 (over z, x), inner: 4 (over y, core).
Axes of the slice: x: 2, y: 2, z: 4, core: 2. Of those that a mesh axis runs over, the one named last changes fastest.
Arguments:
- images: bfloat16 [32, 14, 14, 768], P(('outer', 'inner')), may hold values from -6 to 6
- cotangent: bfloat16 [32, 14, 14, 768], P(('outer', 'inner')), may hold values from -20 to 20
- conv_weight: float32 [7, 7, 768], replicated, may hold values from -0.875 to 0.875
- conv_bias: float32 [768], replicated, may hold values from -3 to 3
- norm_gain: float32 [768], replicated, may hold values from 0.1 to 1.9
- norm_bias: float32 [768], replicated, may hold values from -2 to 2
- expand_weight: bfloat16 [768, 3072], replicated, may hold values from -0.21875 to 0.21875
- expand_bias: float32 [3072], replicated, may hold values from -3 to 3
- reduce_weight: bfloat16 [3072, 768], replicated, may hold values from -0.109375 to 0.109375
- layer_scale: float32 [768], replicated, may hold values from 0.2 to 2
- right_first: float32 [3072, 32], replicated, may hold values from -5 to 5
- right_second: float32 [768, 32], replicated, may hold values from -5 to 5
Outputs:
- next_first: float32 [3072, 32], replicated
- next_second: float32 [768, 32], replicated
All inputs are finite; a program needn't handle non-finite values.
Results may differ from a plain program's by a relative error of at most 0.009.
Values may be sent and summed in bfloat16 or wider, within the bound.
No kernel may reach another device: no remote copies, remote signals or barrier semaphores. Data moves between devices by JAX's collectives and lax.ppermute only.
A program may use at most 64 MiB of HBM per device.

v0:
```python
import jax
import jax.numpy as jnp
from jax import lax
from jax.sharding import PartitionSpec as P


def depthwise(images, conv_weight, conv_bias):
    kernel = conv_weight.shape[0]
    margin = kernel // 2
    extent = images.shape[1]
    widened = jnp.pad(
        images.astype(jnp.float32), ((0, 0), (margin, margin), (margin, margin), (0, 0))
    )
    summed = jnp.zeros(images.shape, jnp.float32) + conv_bias
    for tap_row in range(kernel):
        for tap_col in range(kernel):
            summed = (
                summed
                + widened[:, tap_row : tap_row + extent, tap_col : tap_col + extent, :]
                * conv_weight[tap_row, tap_col]
            )
    return summed


def layer_norm(values, norm_gain, norm_bias):
    center = jnp.mean(values, axis=-1, keepdims=True)
    spread = jnp.mean((values - center) ** 2, axis=-1, keepdims=True)
    return ((values - center) * lax.rsqrt(spread + 1e-06) * norm_gain + norm_bias).astype(
        jnp.bfloat16
    )


def gelu_slope(hidden):
    return (
        0.5 * (1.0 + lax.erf(hidden * 0.7071067811865476))
        + hidden * jnp.exp(-0.5 * hidden * hidden) * 0.3989422804014327
    )


def project(rows_left, rows_right, right):
    thin = jnp.dot(
        rows_right, right.astype(jnp.bfloat16), preferred_element_type=jnp.float32
    ).astype(jnp.bfloat16)
    return lax.dot_general(
        rows_left, thin, (((0,), (0,)), ((), ())), preferred_element_type=jnp.float32
    )


def back_project(rows_left, rows_right, basis):
    rounded = basis.astype(jnp.bfloat16)
    thin = jnp.dot(rows_left, rounded, preferred_element_type=jnp.float32).astype(jnp.bfloat16)
    return lax.dot_general(
        rows_right, thin, (((0,), (0,)), ((), ())), preferred_element_type=jnp.float32
    )


def gram_of(partial_value):
    return lax.dot_general(
        partial_value, partial_value, (((0,), (0,)), ((), ())), precision=lax.Precision.HIGHEST
    )


def apply_factor(gram_matrix, partial_value):
    factor = jnp.linalg.cholesky(gram_matrix)
    return jax.scipy.linalg.solve_triangular(factor, partial_value.T, lower=True).T


def refine_layer(partial_value, rows_left, rows_right, scale):
    summed = lax.psum(partial_value, ("outer", "inner"))
    basis = apply_factor(gram_of(summed), summed)
    term = back_project(rows_left, rows_right, basis)
    return lax.psum(term, ("outer", "inner")) * scale


def shards(
    images,
    cotangent,
    conv_weight,
    conv_bias,
    norm_gain,
    norm_bias,
    expand_weight,
    expand_bias,
    reduce_weight,
    layer_scale,
    right_first,
    right_second,
):
    count = lax.axis_size("outer") * lax.axis_size("inner")
    scale = jnp.float32(1.0) / count
    width = images.shape[-1]
    conv_out = depthwise(images, conv_weight, conv_bias).reshape((-1, width))
    normed = layer_norm(conv_out, norm_gain, norm_bias)
    hidden = jnp.dot(normed, expand_weight, preferred_element_type=jnp.float32) + expand_bias
    activated = jax.nn.gelu(hidden, approximate=False).astype(jnp.bfloat16)
    out_grad = (cotangent.reshape((-1, width)).astype(jnp.float32) * layer_scale).astype(
        jnp.bfloat16
    )
    p_second = project(activated, out_grad, right_second)
    back = lax.dot_general(
        out_grad, reduce_weight, (((1,), (1,)), ((), ())), preferred_element_type=jnp.float32
    )
    hid_grad = (back * gelu_slope(hidden)).astype(jnp.bfloat16)
    p_first = project(normed, hid_grad, right_first)
    next_second = refine_layer(p_second, activated, out_grad, scale)
    next_first = refine_layer(p_first, normed, hid_grad, scale)
    return (next_first, next_second)


def solution(mesh):
    in_specs = (
        P(("outer", "inner"), None, None, None),
        P(("outer", "inner"), None, None, None),
        P(),
        P(),
        P(),
        P(),
        P(),
        P(),
        P(),
        P(),
        P(),
        P(),
    )
    out_specs = (P(), P())
    return jax.shard_map(shards, mesh=mesh, in_specs=in_specs, out_specs=out_specs, check_vma=False)
```

profile of v0, /device:TPU:0, one launch (start us, length us, event | category | flops | bytes accessed | tf_op | source)
XLA Modules:
  0.0 326.7 jit_solution(6438249491796293082)
XLA Ops:
  7.2 1.1 slice_reduce_fusion.46
  8.3 1.4 slice_reduce_fusion.48
  9.7 1.4 slice_reduce_fusion.47
  11.1 1.0 convert_element_type.50
  12.2 6.3 %fusion.126 = (f32[14,14]{1,0:T(8,128)S(1)}, f32[1,14,14,768]{3,2,1,0:T(8,128)S(1)}) fusion(f32[768]{0:T(1024)S(1)} %get-tuple-element.50, f32[768]{0:T(1024)S(1)} %get-tuple-element.51, f32[768]{0:T(1024)S(1)} %get-tuple-element.4, f32[768]{0:T(1024)S(1)} %get-tuple-element.5, f32[768]{0:T(1024)S(1)} %get-tuple-element.6, f32[768]{0:T(1024)S(1)} %get-tuple-element.7, ...), kind=kLoop, calls=%fused_computation.256 | loop fusion | flops 14902076 | bytes 1358608 | tf_op jit(solution)/shard_map/reduce_sum | solution.py:26
  19.2 8.0 %fusion.7 = (bf16[196,3072]{1,0:T(8,128)(2,1)S(1)}, f32[196,3072]{1,0:T(8,128)S(1)}) fusion(f32[3072]{0:T(1024)S(1)} %copy-done.7, bf16[768,3072]{1,0:T(8,128)(2,1)} %param.19, f32[196,768]{1,0:T(8,128)S(1)} %reshape.211, f32[768]{0:T(1024)S(1)} %copy-done.3, f32[768]{0:T(1024)S(1)} %copy-done.4, f32[196]{0:T(256)S(1)} %rsqrt.12, f32[196]{0:T(256)S(1)} %div.15), kind=kOutput, calls=%fused_computation.60 | convolution fusion | flops 965336064 | bytes 8953376 | tf_op jit(solution)/shard_map/dot_general | solution.py:94
  27.2 2.0 fusion
  29.2 2.4 fusion.15
  31.6 1.4 fusion.17
  33.3 130.9 %all-reduce.8.cloned.1.call-done = (f32[768,32]{0,1:T(8,128)}, f32[3072,32]{0,1:T(8,128)}) async-done(((f32[768,32]{0,1:T(8,128)}, f32[3072,32]{0,1:T(8,128)}), (f32[768,32]{0,1:T(8,128)}, f32[3072,32]{0,1:T(8,128)})) %all-reduce.8.cloned.1.call-update) | async-done | bytes 491536 | tf_op jit(solution)/shard_map/psum | solution.py:69
  164.2 1.3 fusion.128
  165.5 1.6 fusion.129
  167.1 2.9 cholesky.55
  170.7 0.7 fusion.121
  171.4 2.4 custom-call.11
  173.8 2.2 convolution_convert_fusion
  176.0 2.3 fusion.16
  178.4 2.9 cholesky.44
  182.6 2.4 custom-call.10
  185.1 0.8 convolution_convert_fusion.1
  185.9 2.1 fusion.18
  188.1 128.5 %all-reduce.6.cloned.1.call-done = (f32[3072,32]{0,1:T(8,128)}, f32[768,32]{0,1:T(8,128)}) async-done(((f32[3072,32]{0,1:T(8,128)}, f32[768,32]{0,1:T(8,128)}), (f32[3072,32]{0,1:T(8,128)}, f32[768,32]{0,1:T(8,128)})) %all-reduce.6.cloned.1.call-update) | async-done | bytes 491536 | tf_op jit(solution)/shard_map/psum | solution.py:72
  316.6 1.8 broadcast_multiply_fusion
  318.3 1.5 broadcast_multiply_fusion.1
  (42 shorter events, 3.1 us)
Async XLA Ops:
  7.2 157.0 %all-reduce.8.cloned.1.call-start = ((), (), s32[]{:S(2)}) async-start(), calls=%async_computation.1 | async-start | bytes 983040 | tf_op jit(solution)/shard_map/psum | solution.py:69
  9.7 9.2 %copy-start.1 = (bf16[1,14,14,768]{3,2,1,0:T(8,128)(2,1)S(1)}, bf16[1,14,14,768]{3,2,1,0:T(8,128)(2,1)}, u32[]{:S(2)}) copy-start(bf16[1,14,14,768]{3,2,1,0:T(8,128)(2,1)} %param.14) | copy-start | bytes 903172
  12.1 6.9 %copy-start.6 = (f32[768]{0:T(1024)S(1)}, f32[768]{0:T(1024)}, u32[]{:S(2)}) copy-start(f32[768]{0:T(1024)} %param.22) | copy-start | bytes 9220
  12.1 7.0 %copy-start.3 = (f32[768]{0:T(1024)S(1)}, f32[768]{0:T(1024)}, u32[]{:S(2)}) copy-start(f32[768]{0:T(1024)} %param.18) | copy-start | bytes 9220
  12.1 7.0 %copy-start.4 = (f32[768]{0:T(1024)S(1)}, f32[768]{0:T(1024)}, u32[]{:S(2)}) copy-start(f32[768]{0:T(1024)} %param.17) | copy-start | bytes 9220
  12.1 7.0 %copy-start.7 = (f32[3072]{0:T(1024)S(1)}, f32[3072]{0:T(1024)}, u32[]{:S(2)}) copy-start(f32[3072]{0:T(1024)} %param.20) | copy-start | bytes 36868
  19.0 10.2 %copy-start.5 = (f32[196]{0:T(256)}, f32[196]{0:T(256)S(1)}, u32[]{:S(2)}) copy-start(f32[196]{0:T(256)S(1)} %rsqrt.12) | copy-start | bytes 2356
  19.1 8.1 %slice-start = ((s8[4718592]{0:T(1024)(128)(4,1)}), s8[4194304]{0:T(1024)(128)(4,1)S(1)}, s32[]{:S(2)}) async-start(s8[4718592]{0:T(1024)(128)(4,1)} %bitcast.35), calls=%async_computation.2 | async-start | bytes 8388608
  19.1 8.1 %slice-start.1 = ((s8[4718592]{0:T(1024)(128)(4,1)}), s8[524288]{0:T(1024)(128)(4,1)S(1)}, s32[]{:S(2)}) async-start(s8[4718592]{0:T(1024)(128)(4,1)} %bitcast.35), calls=%async_computation.3 | async-start | bytes 1048576
  27.2 4.4 %copy-start.2 = (f32[768,32]{0,1:T(8,128)S(1)}, f32[768,32]{0,1:T(8,128)}, u32[]{:S(2)}) copy-start(f32[768,32]{0,1:T(8,128)} %param.24) | copy-start | bytes 294916
  33.1 283.5 %all-reduce.6.cloned.1.call-start = ((), (), s32[]{:S(2)}) async-start(), calls=%async_computation | async-start | bytes 983040 | tf_op jit(solution)/shard_map/psum | solution.py:72
  164.2 20.9 %copy-start = (f32[768,32]{0,1:T(8,128)S(1)}, f32[768,32]{0,1:T(8,128)}, u32[]{:S(2)}) copy-start(f32[768,32]{0,1:T(8,128)} %get-tuple-element.54) | copy-start | bytes 294916
Sparse Core Ops, SparseCore 0:
  33.2 130.9 all-reduce.7
  188.2 128.3 all-reduce.5
where the time goes:
time: 327 us
  waiting for transfers between devices  259 us (79%)
  other arithmetic  24.2 us (7%)
  matrix products  24.1 us (7%)
  between operations  14.3 us (4%)
  local copies, waits for them, and re-layouts  4.39 us (1%)
    psum x1, waiting for transfers between devices, refine_layer(): summed = lax.psum(partial_value, ('outer', 'inner'))  131 us
    psum x1, waiting for transfers between devices, refine_layer(): return lax.psum(term, ('outer', 'inner')) * scale  129 us
    dot_general x1, matrix products, shards(): jnp.dot(normed, expand_weight, preferred_element_type=jnp.float32)  8.02 us
    another operation x6, other arithmetic, apply_factor(): factor = jnp.linalg.cholesky(gram_matrix)  7.19 us
  transfers between devices with their start and end apart: 2, of which 2 were waited for; matrix products, arithmetic and copies ran while one was open for 0% of the time, Pallas kernels for 0%

commit v1 on v0

--- a/solution.py
+++ b/solution.py
@@ -69,7 +69,7 @@
     summed = lax.psum(partial_value, ("outer", "inner"))
     basis = apply_factor(gram_of(summed), summed)
     term = back_project(rows_left, rows_right, basis)
-    return lax.psum(term, ("outer", "inner")) * scale
+    return lax.psum(lax.psum(term, "inner"), "outer") * scale
 
 
 def shards(

time: 327 us -> 308 us (0.942)
  waiting for transfers between devices: 259 us -> 241 us
    psum x1 -> x2, waiting for transfers between devices: 129 us -> 110 us  [refine_layer(): return lax.psum(lax.psum(term, 'inner'), 'outer') * scale]
  transfers between devices with their start and end apart: 2 -> 3, of which waited for: 2 -> 3; matrix products, arithmetic and copies ran while one was open for 0% -> 0% of each run, Pallas kernels for 0% -> 0%
where the time goes in v1:
time: 308 us
  waiting for transfers between devices  241 us (78%)
  other arithmetic  24.2 us (8%)
  matrix products  24.1 us (8%)
  between operations  14 us (5%)
  local copies, waits for them, and re-layouts  4.39 us (1%)
    psum x1, waiting for transfers between devices, refine_layer(): summed = lax.psum(partial_value, ('outer', 'inner'))  131 us
    psum x2, waiting for transfers between devices, refine_layer(): return lax.psum(lax.psum(term, 'inner'), 'outer') * scale  110 us
    dot_general x1, matrix products, shards(): jnp.dot(normed, expand_weight, preferred_element_type=jnp.float32)  8.02 us
    another operation x6, other arithmetic, apply_factor(): factor = jnp.linalg.cholesky(gram_matrix)  7.19 us
    reduce_sum x1, other arithmetic, layer_norm(): center = jnp.mean(values, axis=-1, keepdims=True)  6.22 us
    another operation x4, other arithmetic, apply_factor(): jax.scipy.linalg.solve_triangular(factor, partial_value.T, lower=True)  6.17 us
  transfers between devices with their start and end apart: 3, of which 3 were waited for; matrix products, arithmetic and copies ran while one was open for 0% of the time, Pallas kernels for 0%

profile of v1, /device:TPU:0, one launch (start us, length us, event | category | flops | bytes accessed | tf_op | source)
XLA Modules:
  0.0 307.8 jit_solution(3893757241460512935)
XLA Ops:
  7.2 1.1 slice_reduce_fusion.46
  8.3 1.4 slice_reduce_fusion.48
  9.7 1.4 slice_reduce_fusion.47
  11.1 1.0 convert_element_type.50
  12.2 6.2 %fusion.126 = (f32[14,14]{1,0:T(8,128)S(1)}, f32[1,14,14,768]{3,2,1,0:T(8,128)S(1)}) fusion(f32[768]{0:T(1024)S(1)} %get-tuple-element.50, f32[768]{0:T(1024)S(1)} %get-tuple-element.51, f32[768]{0:T(1024)S(1)} %get-tuple-element.4, f32[768]{0:T(1024)S(1)} %get-tuple-element.5, f32[768]{0:T(1024)S(1)} %get-tuple-element.6, f32[768]{0:T(1024)S(1)} %get-tuple-element.7, ...), kind=kLoop, calls=%fused_computation.256 | loop fusion | flops 14902076 | bytes 1358608 | tf_op jit(solution)/shard_map/reduce_sum | solution.py:26
  19.1 8.0 %fusion.7 = (bf16[196,3072]{1,0:T(8,128)(2,1)S(1)}, f32[196,3072]{1,0:T(8,128)S(1)}) fusion(f32[3072]{0:T(1024)S(1)} %copy-done.7, bf16[768,3072]{1,0:T(8,128)(2,1)} %param.19, f32[196,768]{1,0:T(8,128)S(1)} %reshape.211, f32[768]{0:T(1024)S(1)} %copy-done.3, f32[768]{0:T(1024)S(1)} %copy-done.4, f32[196]{0:T(256)S(1)} %rsqrt.12, f32[196]{0:T(256)S(1)} %div.15), kind=kOutput, calls=%fused_computation.60 | convolution fusion | flops 965336064 | bytes 8953376 | tf_op jit(solution)/shard_map/dot_general | solution.py:94
  27.2 2.0 fusion
  29.2 2.4 fusion.15
  31.6 1.4 fusion.17
  33.1 131.1 %all-reduce.8.cloned.1.call-done = (f32[768,32]{0,1:T(8,128)}, f32[3072,32]{0,1:T(8,128)}) async-done(((f32[768,32]{0,1:T(8,128)}, f32[3072,32]{0,1:T(8,128)}), (f32[768,32]{0,1:T(8,128)}, f32[3072,32]{0,1:T(8,128)})) %all-reduce.8.cloned.1.call-update) | async-done | bytes 491536 | tf_op jit(solution)/shard_map/psum | solution.py:69
  164.3 1.3 fusion.128
  165.5 1.6 fusion.129
  167.2 2.9 cholesky.55
  171.4 2.4 custom-call.11
  173.9 2.2 convolution_convert_fusion
  176.1 2.3 fusion.16
  178.4 2.9 cholesky.44
  182.7 2.4 custom-call.10
  185.1 0.8 convolution_convert_fusion.1
  186.0 2.1 fusion.18
  188.2 33.7 %all-reduce.12.cloned.1.call-done = (f32[3072,32]{0,1:T(8,128)}, f32[768,32]{0,1:T(8,128)}) async-done(((f32[3072,32]{0,1:T(8,128)}, f32[768,32]{0,1:T(8,128)}), (f32[3072,32]{0,1:T(8,128)}, f32[768,32]{0,1:T(8,128)})) %all-reduce.12.cloned.1.call-update) | async-done | bytes 491536 | tf_op jit(solution)/shard_map/psum | solution.py:72
  221.9 76.1 %all-reduce.10.cloned.1.call-done = (f32[3072,32]{0,1:T(8,128)}, f32[768,32]{0,1:T(8,128)}) async-done(((f32[3072,32]{0,1:T(8,128)}, f32[768,32]{0,1:T(8,128)}), (f32[3072,32]{0,1:T(8,128)}, f32[768,32]{0,1:T(8,128)})) %all-reduce.10.cloned.1.call-update) | async-done | bytes 491536 | tf_op jit(solution)/shard_map/psum | solution.py:72
  298.0 1.8 broadcast_multiply_fusion
  299.8 1.5 broadcast_multiply_fusion.1
  (45 shorter events, 3.7 us)
Async XLA Ops:
  7.2 157.1 %all-reduce.8.cloned.1.call-start = ((), (), s32[]{:S(2)}) async-start(), calls=%async_computation | async-start | bytes 983040 | tf_op jit(solution)/shard_map/psum | solution.py:69
  9.7 9.1 %copy-start.1 = (bf16[1,14,14,768]{3,2,1,0:T(8,128)(2,1)S(1)}, bf16[1,14,14,768]{3,2,1,0:T(8,128)(2,1)}, u32[]{:S(2)}) copy-start(bf16[1,14,14,768]{3,2,1,0:T(8,128)(2,1)} %param.14) | copy-start | bytes 903172
  12.1 6.9 %copy-start.6 = (f32[768]{0:T(1024)S(1)}, f32[768]{0:T(1024)}, u32[]{:S(2)}) copy-start(f32[768]{0:T(1024)} %param.22) | copy-start | bytes 9220
  12.1 7.0 %copy-start.3 = (f32[768]{0:T(1024)S(1)}, f32[768]{0:T(1024)}, u32[]{:S(2)}) copy-start(f32[768]{0:T(1024)} %param.18) | copy-start | bytes 9220
  12.1 7.0 %copy-start.4 = (f32[768]{0:T(1024)S(1)}, f32[768]{0:T(1024)}, u32[]{:S(2)}) copy-start(f32[768]{0:T(1024)} %param.17) | copy-start | bytes 9220
  12.1 7.0 %copy-start.7 = (f32[3072]{0:T(1024)S(1)}, f32[3072]{0:T(1024)}, u32[]{:S(2)}) copy-start(f32[3072]{0:T(1024)} %param.20) | copy-start | bytes 36868
  19.0 10.2 %copy-start.5 = (f32[196]{0:T(256)}, f32[196]{0:T(256)S(1)}, u32[]{:S(2)}) copy-start(f32[196]{0:T(256)S(1)} %rsqrt.12) | copy-start | bytes 2356
  19.0 8.1 %slice-start = ((s8[4718592]{0:T(1024)(128)(4,1)}), s8[4194304]{0:T(1024)(128)(4,1)S(1)}, s32[]{:S(2)}) async-start(s8[4718592]{0:T(1024)(128)(4,1)} %bitcast.35), calls=%async_computation.3 | async-start | bytes 8388608
  19.1 8.1 %slice-start.1 = ((s8[4718592]{0:T(1024)(128)(4,1)}), s8[524288]{0:T(1024)(128)(4,1)S(1)}, s32[]{:S(2)}) async-start(s8[4718592]{0:T(1024)(128)(4,1)} %bitcast.35), calls=%async_computation.4 | async-start | bytes 1048576
  27.2 4.4 %copy-start.2 = (f32[768,32]{0,1:T(8,128)S(1)}, f32[768,32]{0,1:T(8,128)}, u32[]{:S(2)}) copy-start(f32[768,32]{0,1:T(8,128)} %param.24) | copy-start | bytes 294916
  33.1 188.8 %all-reduce.12.cloned.1.call-start = ((), (), s32[]{:S(2)}) async-start(), calls=%async_computation.2 | async-start | bytes 983040 | tf_op jit(solution)/shard_map/psum | solution.py:72
  164.3 20.9 %copy-start = (f32[768,32]{0,1:T(8,128)S(1)}, f32[768,32]{0,1:T(8,128)}, u32[]{:S(2)}) copy-start(f32[768,32]{0,1:T(8,128)} %get-tuple-element.52) | copy-start | bytes 294916
  188.1 109.9 %all-reduce.10.cloned.1.call-start = ((), (), s32[]{:S(2)}) async-start(), calls=%async_computation.1 | async-start | bytes 983040 | tf_op jit(solution)/shard_map/psum | solution.py:72
Sparse Core Ops, SparseCore 0:
  33.2 131.0 all-reduce.7
  188.2 33.5 all-reduce.11
  225.3 72.6 all-reduce.9
